TPU v7x, 32 devices: a whole 2x2x4 slice. The times are simulated.
32 devices in a mesh: dom: 8 (over z, y), batch: 4 (over x, core).
Axes of the slice: x: 2, y: 2, z: 4, core: 2. Of those that a mesh axis runs over, the one named last changes fastest.
Arguments:
- signal: bfloat16 [4096, 4, 4, 256], P('dom', 'batch'), may hold values from -6 to 6
- cotangent: bfloat16 [4096, 4, 3, 256], P('dom', 'batch'), may hold values from -6 to 6
- conv_weight: bfloat16 [2, 2, 256, 256], replicated, may hold values from -0.25 to 0.25
- mix_weight: bfloat16 [3, 256, 256], replicated, may hold values from -0.21875 to 0.21875
- send_rows: int32 [64, 16], P('dom'), may hold values from 0 to 511
- send_mask: int32 [64, 16], P('dom'), may hold values 0 or 1
- tile_vals: bfloat16 [128, 128, 128], P('dom'), may hold values from -0.26953125 to 0.26953125
- tile_row: int32 [128], P('dom'), may hold values from 0 to 3
- tile_col: int32 [128], P('dom'), may hold values from 0 to 5
- tile_mask: int32 [128], P('dom'), may hold values 0 or 1
- hub_owner: int32 [8], replicated, may hold values from 0 to 7, as said below
- hub_rows: int32 [8, 16], replicated, may hold values from 0 to 511
Outputs:
- layer_out: bfloat16 [4096, 4, 3, 256], P('dom', 'batch')
- signal_grad: bfloat16 [4096, 4, 4, 256], P('dom', 'batch')
- conv_grad: float32 [2, 2, 256, 256], replicated
- mix_grad: float32 [3, 256, 256], replicated
Inputs may be any that keep to these rules, and one draw needn't show every extreme that they name: `hub_owner`: each owner slot names a different partition.
All inputs are finite; a program needn't handle non-finite values. No bound on the sum of `send_mask` or of `tile_mask` on one device may be relied on, other than what follows from the above.
Results may differ from a plain program's by a relative error of at most 0.0056.
Values may be sent and summed in bfloat16 or wider, within the bound.
A program may use at most 128 MiB of HBM per device.

v0:
```python
import math
import jax
import jax.numpy as jnp
from jax import lax
from jax.sharding import PartitionSpec as P

highest = lax.Precision.HIGHEST


def tile_apply(ext_rows, tile_block, row_ids, col_ids, tile_keep, row_tiles):
    block_rows = tile_block.shape[1]
    features = ext_rows.shape[1]
    chosen = ext_rows.reshape(-1, block_rows, features)[col_ids]
    product = jnp.einsum("tij,tjf->tif", tile_block, chosen, preferred_element_type=jnp.float32)
    product = product * tile_keep[:, None, None]
    onehot = (row_ids[None, :] == jnp.arange(row_tiles, dtype=jnp.int32)[:, None]).astype(
        jnp.float32
    )
    return jnp.einsum("rt,tif->rif", onehot, product, precision=highest).reshape(
        row_tiles * block_rows, features
    )


def tile_back(own_rows, tile_block, row_ids, col_ids, tile_keep, col_tiles):
    block_rows = tile_block.shape[1]
    features = own_rows.shape[1]
    chosen = own_rows.reshape(-1, block_rows, features)[row_ids]
    product = jnp.einsum("tji,tjf->tif", tile_block, chosen, preferred_element_type=jnp.float32)
    product = product * tile_keep[:, None, None]
    onehot = (col_ids[None, :] == jnp.arange(col_tiles, dtype=jnp.int32)[:, None]).astype(
        jnp.float32
    )
    return jnp.einsum("ct,tif->cif", onehot, product, precision=highest).reshape(
        col_tiles * block_rows, features
    )


def mm(left, right):
    return jnp.dot(left, right, preferred_element_type=jnp.float32)


def inner_sum(left, right):
    return lax.dot_general(
        left, right, (((0,), (0,)), ((), ())), preferred_element_type=jnp.float32
    )


def body(
    signal,
    cotangent,
    conv_weight,
    mix_weight,
    send_rows,
    send_mask,
    tile_vals,
    tile_row,
    tile_col,
    tile_mask,
    hub_owner,
    hub_rows,
):
    node_dev, b_dev, steps, chans = signal.shape
    out_steps = steps - 1
    block_rows = tile_vals.shape[1]
    features = b_dev * out_steps * chans
    halo_count = send_rows.shape[0] * send_rows.shape[1]
    hub_count = hub_rows.shape[0] * hub_rows.shape[1]
    ext_count = node_dev + halo_count + hub_count
    my_index = lax.axis_index("dom")
    flat_send = send_rows.reshape(-1)
    send_flag = send_mask.reshape(-1)
    keep_send = send_flag.astype(jnp.bfloat16)
    flat_hub = hub_rows.reshape(-1)
    mine = jnp.repeat(hub_owner, hub_rows.shape[1]) == my_index
    positions = jnp.arange(node_dev, dtype=jnp.int32)
    return_halo = ((positions[:, None] == flat_send[None, :]) & (send_flag[None, :] == 1)).astype(
        jnp.float32
    )
    return_hub = ((positions[:, None] == flat_hub[None, :]) & mine[None, :]).astype(jnp.float32)
    tile_keep = tile_mask.astype(jnp.float32)

    def spread(field):
        outgoing = field[flat_send] * keep_send[:, None]
        incoming = lax.all_to_all(outgoing, "dom", split_axis=0, concat_axis=0, tiled=True)
        placed = jnp.where(
            mine[:, None], field[flat_hub].astype(jnp.float32), jnp.zeros((), jnp.float32)
        )
        hubs = lax.psum(placed, "dom").astype(jnp.bfloat16)
        ext_rows = jnp.concatenate([field, incoming, hubs], 0)
        return tile_apply(
            ext_rows, tile_vals, tile_row, tile_col, tile_keep, node_dev // block_rows
        )

    def gather_back(field):
        ext_grad = tile_back(
            field, tile_vals, tile_row, tile_col, tile_keep, ext_count // block_rows
        )
        returned = lax.all_to_all(
            ext_grad[node_dev : node_dev + halo_count].astype(jnp.bfloat16),
            "dom",
            split_axis=0,
            concat_axis=0,
            tiled=True,
        ).astype(jnp.float32)
        summed = lax.psum(ext_grad[node_dev + halo_count :], "dom")
        local = ext_grad[:node_dev] + jnp.dot(return_halo, returned, precision=highest)
        return local + jnp.dot(return_hub, summed, precision=highest)

    earlier = signal[:, :, :-1, :].reshape(-1, chans)
    later = signal[:, :, 1:, :].reshape(-1, chans)
    filt = mm(earlier, conv_weight[0, 0]) + mm(later, conv_weight[0, 1])
    gate = mm(earlier, conv_weight[1, 0]) + mm(later, conv_weight[1, 1])
    tanh_filt = jnp.tanh(filt)
    sig_gate = jax.nn.sigmoid(gate)
    hidden = (tanh_filt * sig_gate).astype(jnp.bfloat16)
    hop_one = spread(hidden.reshape(node_dev, features)).astype(jnp.bfloat16)
    hop_two = spread(hop_one).astype(jnp.bfloat16)
    hop_one = hop_one.reshape(-1, chans)
    hop_two = hop_two.reshape(-1, chans)
    mixed = (
        later.astype(jnp.float32)
        + mm(hidden, mix_weight[0])
        + mm(hop_one, mix_weight[1])
        + mm(hop_two, mix_weight[2])
    )
    layer_out = mixed.astype(jnp.bfloat16).reshape(node_dev, b_dev, out_steps, chans)
    grad_out = cotangent.reshape(-1, chans)
    mix_part = jnp.stack(
        [inner_sum(hidden, grad_out), inner_sum(hop_one, grad_out), inner_sum(hop_two, grad_out)]
    )
    back_two = mm(grad_out, mix_weight[2].T).astype(jnp.bfloat16)
    back_one = mm(grad_out, mix_weight[1].T) + gather_back(
        back_two.reshape(node_dev, features)
    ).reshape(-1, chans)
    back_one = back_one.astype(jnp.bfloat16)
    grad_hidden = mm(grad_out, mix_weight[0].T) + gather_back(
        back_one.reshape(node_dev, features)
    ).reshape(-1, chans)
    grad_filt = (grad_hidden * sig_gate * (1.0 - tanh_filt * tanh_filt)).astype(jnp.bfloat16)
    grad_gate = (grad_hidden * tanh_filt * sig_gate * (1.0 - sig_gate)).astype(jnp.bfloat16)
    conv_part = jnp.stack(
        [
            jnp.stack([inner_sum(earlier, grad_filt), inner_sum(later, grad_filt)]),
            jnp.stack([inner_sum(earlier, grad_gate), inner_sum(later, grad_gate)]),
        ]
    )
    shape_four = (node_dev, b_dev, out_steps, chans)
    into_earlier = (
        mm(grad_filt, conv_weight[0, 0].T) + mm(grad_gate, conv_weight[1, 0].T)
    ).reshape(shape_four)
    into_later = (
        mm(grad_filt, conv_weight[0, 1].T)
        + mm(grad_gate, conv_weight[1, 1].T)
        + grad_out.astype(jnp.float32)
    ).reshape(shape_four)
    signal_grad = jnp.pad(into_earlier, ((0, 0), (0, 0), (0, 1), (0, 0))) + jnp.pad(
        into_later, ((0, 0), (0, 0), (1, 0), (0, 0))
    )
    conv_total, mix_total = lax.psum((conv_part, mix_part), ("dom", "batch"))
    factor = 1.0 / math.sqrt(
        node_dev * lax.axis_size("dom") * b_dev * lax.axis_size("batch") * out_steps
    )
    return (layer_out, signal_grad.astype(jnp.bfloat16), conv_total * factor, mix_total * factor)


def solution(mesh):
    placed = (
        P("dom", "batch", None, None),
        P("dom", "batch", None, None),
        P(),
        P(),
        P("dom", None),
        P("dom", None),
        P("dom", None, None),
        P("dom"),
        P("dom"),
        P("dom"),
        P(),
        P(),
    )
    return jax.shard_map(
        body,
        mesh=mesh,
        in_specs=placed,
        out_specs=(P("dom", "batch", None, None), P("dom", "batch", None, None), P(), P()),
        check_vma=False,
    )
```

profile of v0, /device:TPU:0, one launch (start us, length us, event | category | flops | bytes accessed | tf_op | source)
XLA Modules:
  0.0 550.8 jit_solution(4992081128185602620)
XLA Ops:
  7.2 1.9 copy.24
  9.8 1.3 convolution_convert_fusion
  11.5 2.4 gather_fusion.6
  14.0 5.6 %fusion.96 = f32[16,768,128]{2,1,0:T(8,128)} fusion(bf16[16,128,768]{2,1,0:T(8,128)(2,1)} %gather_fusion.6, bf16[16,128,128]{2,1,0:T(8,128)(2,1)S(1)} %copy-done), kind=kOutput, calls=%fused_computation.145 | convolution fusion | flops 402653184 | bytes 9961472 | tf_op jit(solution)/shard_map/tji,tjf->tif/dot_general | solution.py:28
  19.5 6.7 %copy.32 = f32[16,768,128]{1,0,2:T(8,128)} copy(f32[16,768,128]{2,1,0:T(8,128)} %fusion.96) | data formatting | bytes 12582912 | tf_op jit(solution)/shard_map/tji,tjf->tif/dot_general | solution.py:28
  26.3 4.6 fusion.2
  30.9 1.6 copy-done.1
  33.8 2.3 slice.168
  36.8 7.3 %all-to-all-start.2 = ((bf16[8,16,768]{2,1,0:T(8,128)(2,1)}), bf16[8,16,768]{2,1,0:T(8,128)(2,1)}, u32[]{:S(2)}, u32[]{:S(2)}) async-start(bf16[8,16,768]{2,1,0:T(8,128)(2,1)} %bitcast.44), calls=%async_computation.2 | async-start | bytes 393216 | tf_op jit(solution)/shard_map/all_to_all | solution.py:98
  44.5 3.3 slice.103
  48.3 3.0 copy.25
  51.4 2.0 fusion.93
  53.5 2.5 reshape.178
  55.9 2.7 reshape.179
  59.1 1.5 fusion.17
  60.6 49.4 %all-reduce.9.cloned.1.call-done = f32[128,768]{1,0:T(8,128)} async-done(((f32[128,768]{1,0:T(8,128)}), f32[128,768]{1,0:T(8,128)}) %all-reduce.9.cloned.1.call-update) | async-done | bytes 393232 | tf_op jit(solution)/shard_map/psum | solution.py:105
  110.0 3.0 fusion.39
  112.9 3.5 fusion.25
  116.4 2.6 reshape.187
  119.0 2.8 fusion.23
  121.8 1.5 reshape_reshape.7
  123.3 2.4 gather_fusion.7
  125.7 5.6 %fusion.97 = f32[16,768,128]{2,1,0:T(8,128)} fusion(bf16[16,128,768]{2,1,0:T(8,128)(2,1)} %gather_fusion.7, bf16[16,128,128]{2,1,0:T(8,128)(2,1)S(1)} %copy-done), kind=kOutput, calls=%fused_computation.146 | convolution fusion | flops 402653184 | bytes 9961472 | tf_op jit(solution)/shard_map/tji,tjf->tif/dot_general | solution.py:28
  131.3 6.7 %copy.33 = f32[16,768,128]{1,0,2:T(8,128)} copy(f32[16,768,128]{2,1,0:T(8,128)} %fusion.97) | data formatting | bytes 12582912 | tf_op jit(solution)/shard_map/tji,tjf->tif/dot_general | solution.py:28
  138.0 4.6 fusion
  142.6 1.6 copy-done.2
  145.4 1.5 fusion.50
  146.9 2.3 slice.167
  149.9 4.1 all-to-all-start.3
  154.1 1.4 slice-done
  155.5 1.5 copy.26
  157.0 60.8 %all-reduce.11.cloned.1.call-done = f32[128,768]{1,0:T(8,128)} async-done(((f32[128,768]{1,0:T(8,128)}), f32[128,768]{1,0:T(8,128)}) %all-reduce.11.cloned.1.call-update) | async-done | bytes 393232 | tf_op jit(solution)/shard_map/psum | solution.py:105
  217.8 3.0 fusion.37
  220.7 3.4 fusion.24
  224.1 2.6 reshape.188
  226.8 2.0 convolution_add_fusion.3
  229.4 1.9 multiply_convert_fusion
  235.8 1.6 fusion.55
  237.4 1.6 fusion.52
  239.4 1.6 gather_fusion.1
  240.9 1.8 convert_select_fusion.1
  242.7 40.9 %all-reduce.14 = bf16[128,768]{1,0:T(8,128)(2,1)} all-reduce(f32[128,768]{1,0:T(8,128)} %convert_select_fusion.1), channel_id=1, replica_groups=mesh['dom'=8,'batch'=4] {'dom'}, use_global_device_ids=true, to_apply=%region_0.1 | all-reduce | flops 98304 | bytes 589824 | tf_op jit(solution)/shard_map/psum | solution.py:88
  283.6 1.5 gather_fusion
  285.1 1.7 broadcast_multiply_fusion.3
  286.8 4.2 all-to-all-start
  291.0 3.4 convolution_add_fusion.1
  294.4 1.6 fusion.16
  297.2 3.6 reshape.189
  300.8 3.6 reshape.190
  304.4 4.0 fusion.32
  310.6 2.4 gather_fusion.2
  313.0 5.6 %fusion.94 = f32[16,768,128]{2,1,0:T(8,128)} fusion(bf16[16,128,768]{2,1,0:T(8,128)(2,1)} %gather_fusion.2, bf16[16,128,128]{2,1,0:T(8,128)(2,1)S(1)} %copy-done), kind=kOutput, calls=%fused_computation.143 | convolution fusion | flops 402653184 | bytes 9961472 | tf_op jit(solution)/shard_map/tij,tjf->tif/dot_general | solution.py:14
  318.6 6.7 %copy.30 = f32[16,768,128]{1,0,2:T(8,128)} copy(f32[16,768,128]{2,1,0:T(8,128)} %fusion.94) | data formatting | bytes 12582912 | tf_op jit(solution)/shard_map/tij,tjf->tif/dot_general | solution.py:14
  325.3 5.6 %fusion.26 = bf16[4,128,768]{2,0,1:T(4,128)(2,1)S(1)} fusion(f32[16,768,128]{1,0,2:T(8,128)} %copy.30, f32[16]{0:T(128)S(1)} %convert_element_type.95, s32[16]{0:T(128)S(1)} %copy-done.30), kind=kOutput, calls=%fused_computation.50 | convolution fusion | flops 77463616 | bytes 7078016 | tf_op jit(solution)/shard_map/rt,tif->rif/dot_general | solution.py:19
  331.0 1.5 gather_fusion.4
  335.8 6.0 %all-to-all-start.1 = ((bf16[8,16,768]{2,1,0:T(8,128)(2,1)}), bf16[8,16,768]{2,1,0:T(8,128)(2,1)S(1)}, u32[]{:S(2)}, u32[]{:S(2)}) async-start(bf16[8,16,768]{2,1,0:T(8,128)(2,1)} %broadcast_multiply_fusion.2), calls=%async_computation.1 | async-start | bytes 393216 | tf_op jit(solution)/shard_map/all_to_all | solution.py:84
  341.8 42.5 %all-reduce.15 = bf16[128,768]{1,0:T(8,128)(2,1)} all-reduce(f32[128,768]{1,0:T(8,128)S(1)} %convert_select_fusion), channel_id=1, replica_groups=mesh['dom'=8,'batch'=4] {'dom'}, use_global_device_ids=true, to_apply=%region_1.2 | all-reduce | flops 98304 | bytes 589824 | tf_op jit(solution)/shard_map/psum | solution.py:88
  386.4 2.4 gather_fusion.5
  388.8 5.6 %fusion.95 = f32[16,768,128]{2,1,0:T(8,128)} fusion(bf16[16,128,768]{2,1,0:T(8,128)(2,1)} %gather_fusion.5, bf16[16,128,128]{2,1,0:T(8,128)(2,1)S(1)} %copy-done), kind=kOutput, calls=%fused_computation.144 | convolution fusion | flops 402653184 | bytes 9961472 | tf_op jit(solution)/shard_map/tij,tjf->tif/dot_general | solution.py:14
  394.4 6.7 %copy.31 = f32[16,768,128]{1,0,2:T(8,128)} copy(f32[16,768,128]{2,1,0:T(8,128)} %fusion.95) | data formatting | bytes 12582912 | tf_op jit(solution)/shard_map/tij,tjf->tif/dot_general | solution.py:14
  401.1 5.6 %fusion.29 = bf16[4,128,768]{2,0,1:T(4,128)(2,1)S(1)} fusion(f32[16,768,128]{1,0,2:T(8,128)} %copy.31, f32[16]{0:T(128)S(1)} %convert_element_type.95, s32[16]{0:T(128)S(1)} %copy-done.30), kind=kOutput, calls=%fused_computation.51 | convolution fusion | flops 77463616 | bytes 7078016 | tf_op jit(solution)/shard_map/rt,tif->rif/dot_general | solution.py:19
  413.2 127.3 %all-reduce.13.cloned.1.call-done = (f32[2,2,256,256]{2,3,1,0:T(8,128)}, f32[3,256,256]{2,1,0:T(8,128)}) async-done(((f32[2,2,256,256]{2,3,1,0:T(8,128)}, f32[3,256,256]{2,1,0:T(8,128)}), (f32[2,2,256,256]{2,3,1,0:T(8,128)}, f32[3,256,256]{2,1,0:T(8,128)})) %all-reduce.13.cloned.1.call-update) | async-done | bytes 1835024 | tf_op jit(solution)/shard_map/psum | solution.py:159
  540.5 1.3 broadcast_multiply_fusion
  541.8 1.3 copy.29
  (129 shorter events, 27.8 us)
Async XLA Ops:
  7.2 6.8 %copy-start = (bf16[16,128,128]{2,1,0:T(8,128)(2,1)S(1)}, bf16[16,128,128]{2,1,0:T(8,128)(2,1)}, u32[]{:S(2)}) copy-start(bf16[16,128,128]{2,1,0:T(8,128)(2,1)} %param.18) | copy-start | bytes 1572868
  7.2 102.8 %all-reduce.9.cloned.1.call-start = ((), (), s32[]{:S(2)}) async-start(), calls=%async_computation.4 | async-start | bytes 786432 | tf_op jit(solution)/shard_map/psum | solution.py:105
  9.8 1.7 copy-start.30
  19.5 6.7 %copy-start.31 = (s32[16]{0:T(128)S(1)}, s32[16]{0:T(128)}, u32[]{:S(2)}) copy-start(s32[16]{0:T(128)} %param.21) | copy-start | bytes 196
  19.5 6.7 %copy-start.29 = (s32[16]{0:T(128)S(1)}, s32[16]{0:T(128)}, u32[]{:S(2)}) copy-start(s32[16]{0:T(128)} %param.20) | copy-start | bytes 196
  30.9 1.6 copy-start.1
  36.8 76.2 %all-to-all-start.2 = ((bf16[8,16,768]{2,1,0:T(8,128)(2,1)}), bf16[8,16,768]{2,1,0:T(8,128)(2,1)}, u32[]{:S(2)}, u32[]{:S(2)}) async-start(bf16[8,16,768]{2,1,0:T(8,128)(2,1)} %bitcast.44), calls=%async_computation.2 | async-start | bytes 393216 | tf_op jit(solution)/shard_map/all_to_all | solution.py:98
  44.1 173.7 %all-reduce.11.cloned.1.call-start = ((), (), s32[]{:S(2)}) async-start(), calls=%async_computation.5 | async-start | bytes 786432 | tf_op jit(solution)/shard_map/psum | solution.py:105
  44.4 3.4 copy-start.27
  44.4 3.5 copy-start.28
  44.4 3.7 copy-start.26
  44.5 3.7 copy-start.32
  48.3 3.1 copy-start.7
  53.5 5.2 copy-start.14
  55.9 3.1 copy-start.3
  142.6 1.6 copy-start.2
  149.9 70.8 %all-to-all-start.3 = ((bf16[8,16,768]{2,1,0:T(8,128)(2,1)}), bf16[8,16,768]{2,1,0:T(8,128)(2,1)S(1)}, u32[]{:S(2)}, u32[]{:S(2)}) async-start(bf16[8,16,768]{2,1,0:T(8,128)(2,1)} %bitcast.46), calls=%async_computation.3 | async-start | bytes 393216 | tf_op jit(solution)/shard_map/all_to_all | solution.py:98
  154.1 1.4 slice-start
  226.8 2.0 copy-start.4
  226.8 2.2 copy-start.15
  226.8 2.7 copy-start.17
  231.4 2.2 copy-start.10
  237.4 1.6 copy-start.8
  286.8 22.7 %all-to-all-start = ((bf16[8,16,768]{2,1,0:T(8,128)(2,1)}), bf16[8,16,768]{2,1,0:T(8,128)(2,1)}, u32[]{:S(2)}, u32[]{:S(2)}) async-start(bf16[8,16,768]{2,1,0:T(8,128)(2,1)} %broadcast_multiply_fusion.3), calls=%async_computation | async-start | bytes 393216 | tf_op jit(solution)/shard_map/all_to_all | solution.py:84
  291.0 3.4 copy-start.6
  291.0 3.4 copy-start.11
  294.4 1.6 copy-start.22
  294.4 1.6 copy-start.23
  294.4 1.6 copy-start.24
  294.4 1.6 copy-start.25
  308.4 1.1 copy-start.19
  333.8 51.6 %copy-start.12 = (bf16[1536,256]{1,0:T(8,128)(2,1)}, bf16[1536,256]{1,0:T(8,128)(2,1)S(1)}, u32[]{:S(2)}) copy-start(bf16[1536,256]{1,0:T(8,128)(2,1)S(1)} %convert_element_type.97) | copy-start | bytes 2359300
  335.8 49.6 %all-to-all-start.1 = ((bf16[8,16,768]{2,1,0:T(8,128)(2,1)}), bf16[8,16,768]{2,1,0:T(8,128)(2,1)S(1)}, u32[]{:S(2)}, u32[]{:S(2)}) async-start(bf16[8,16,768]{2,1,0:T(8,128)(2,1)} %broadcast_multiply_fusion.2), calls=%async_computation.1 | async-start | bytes 393216 | tf_op jit(solution)/shard_map/all_to_all | solution.py:84
  341.8 198.7 %all-reduce.13.cloned.1.call-start = ((), (), s32[]{:S(2)}) async-start(), calls=%async_computation.6 | async-start | bytes 3670016 | tf_op jit(solution)/shard_map/psum | solution.py:159
  406.8 1.0 copy-start.20
  407.2 1.0 copy-start.21
  408.2 1.4 copy-start.5
  408.2 1.7 copy-start.9
  408.2 1.7 copy-start.16
  409.9 1.1 copy-start.13
  541.8 1.3 copy-start.18
Sparse Core Ops, SparseCore 0:
  33.9 76.0 all-reduce.8
  145.6 72.1 all-reduce.10
  409.3 131.1 all-reduce.12
where the time goes:
time: 557 us; the launch traced here: 551 us
  waiting for transfers between devices  238 us (43%)
  local copies, waits for them, and re-layouts  94.4 us (17%)
  blocking collectives  83.3 us (15%)
  matrix products  83.2 us (15%)
  starting transfers between devices  22 us (4%)
  other arithmetic  15.9 us (3%)
  between operations  14.5 us (3%)
    psum x1, waiting for transfers between devices, body(): conv_total, mix_total = lax.psum((conv_part, mix_part), ('dom', 'batch'))  127 us
    psum x2, waiting for transfers between devices, gather_back(): summed = lax.psum(ext_grad[node_dev + halo_count:], 'dom')  110 us
    psum x2, blocking collectives, spread(): hubs = lax.psum(placed, 'dom').astype(jnp.bfloat16)  83.3 us
    dot_general x14, matrix products, mm(): return jnp.dot(left, right, preferred_element_type=jnp.float32)  20.6 us
    dot_general x2, local copies, waits for them, and re-layouts, tile_back(): jnp.einsum('tji,tjf->tif', tile_block, chosen, preferred_element_type=jnp...  13.4 us
    dot_general x2, local copies, waits for them, and re-layouts, tile_apply(): jnp.einsum('tij,tjf->tif', tile_block, chosen, preferred_element_type=jnp...  13.4 us
    unnamed x73, local copies, waits for them, and re-layouts  13.2 us
    all_to_all x2, starting transfers between devices, gather_back(): lax.all_to_all(ext_grad[node_dev:node_dev + halo_count].astype(jnp.bfloat...  11.4 us
  transfers between devices with their start and end apart: 7, of which 3 were waited for; matrix products, arithmetic and copies ran while one was open for 10% of the time, Pallas kernels for 0%

commit v1 on v0

--- a/solution.py
+++ b/solution.py
@@ -5,6 +5,11 @@
 from jax.sharding import PartitionSpec as P
 
 highest = lax.Precision.HIGHEST
+
+
+def one_after_other(value, axis_one, axis_two):
+    partial = lax.psum(value, axis_one)
+    return lax.psum(partial, axis_two)
 
 
 def tile_apply(ext_rows, tile_block, row_ids, col_ids, tile_keep, row_tiles):
@@ -156,7 +161,7 @@
     signal_grad = jnp.pad(into_earlier, ((0, 0), (0, 0), (0, 1), (0, 0))) + jnp.pad(
         into_later, ((0, 0), (0, 0), (1, 0), (0, 0))
     )
-    conv_total, mix_total = lax.psum((conv_part, mix_part), ("dom", "batch"))
+    conv_total, mix_total = one_after_other((conv_part, mix_part), "batch", "dom")
     factor = 1.0 / math.sqrt(
         node_dev * lax.axis_size("dom") * b_dev * lax.axis_size("batch") * out_steps
     )

time: 557 us -> 549 us (0.986)
    psum x1 -> x2, waiting for transfers between devices: 127 us -> 122 us  [the longest x1 79.4 us: one_after_other(): return lax.psum(partial, axis_two)]
    unnamed x73 -> x71, local copies, waits for them, and re-layouts: 13.2 us -> 14.2 us
  transfers between devices with their start and end apart: 7 -> 8, of which waited for: 3 -> 5; matrix products, arithmetic and copies ran while one was open for 10% -> 10% of each run, Pallas kernels for 0% -> 0%
where the time goes in v1:
time: 549 us; the launch traced here: 543 us
  waiting for transfers between devices  236 us (43%)
  local copies, waits for them, and re-layouts  95.8 us (17%)
  blocking collectives  82.8 us (15%)
  matrix products  81.2 us (15%)
  starting transfers between devices  18.5 us (3%)
  between operations  14.6 us (3%)
  other arithmetic  13.8 us (3%)
    psum x2, waiting for transfers between devices, gather_back(): summed = lax.psum(ext_grad[node_dev + halo_count:], 'dom')  110 us
    psum x2, blocking collectives, spread(): hubs = lax.psum(placed, 'dom').astype(jnp.bfloat16)  82.8 us
    psum x1, waiting for transfers between devices, one_after_other(): return lax.psum(partial, axis_two)  79.4 us
    psum x1, waiting for transfers between devices, one_after_other(): partial = lax.psum(value, axis_one)  42.5 us
    dot_general x14, matrix products, mm(): return jnp.dot(left, right, preferred_element_type=jnp.float32)  19.3 us
    unnamed x71, local copies, waits for them, and re-layouts  14.2 us
    dot_general x2, local copies, waits for them, and re-layouts, tile_back(): jnp.einsum('tji,tjf->tif', tile_block, chosen, preferred_element_type=jnp...  13.8 us
    dot_general x2, local copies, waits for them, and re-layouts, tile_apply(): jnp.einsum('tij,tjf->tif', tile_block, chosen, preferred_element_type=jnp...  13.7 us
  transfers between devices with their start and end apart: 8, of which 5 were waited for; matrix products, arithmetic and copies ran while one was open for 10% of the time, Pallas kernels for 0%

profile of v1, /device:TPU:0, one launch (start us, length us, event | category | flops | bytes accessed | tf_op | source)
XLA Modules:
  0.0 542.7 jit_solution(10576025521813002492)
XLA Ops:
  7.2 1.9 copy.24
  9.8 1.3 convolution_convert_fusion
  11.5 2.4 gather_fusion.6
  13.9 5.6 %fusion.96 = f32[16,768,128]{2,1,0:T(8,128)} fusion(bf16[16,128,768]{2,1,0:T(8,128)(2,1)} %gather_fusion.6, bf16[16,128,128]{2,1,0:T(8,128)(2,1)S(1)} %copy-done), kind=kOutput, calls=%fused_computation.145 | convolution fusion | flops 402653184 | bytes 9961472 | tf_op jit(solution)/shard_map/tji,tjf->tif/dot_general | solution.py:33
  19.6 6.9 %copy.32 = f32[16,768,128]{1,0,2:T(8,128)} copy(f32[16,768,128]{2,1,0:T(8,128)} %fusion.96) | data formatting | bytes 12582912 | tf_op jit(solution)/shard_map/tji,tjf->tif/dot_general | solution.py:33
  26.5 4.6 fusion.2
  31.1 1.6 copy-done.1
  33.9 2.3 slice.168
  36.9 7.3 %all-to-all-start.2 = ((bf16[8,16,768]{2,1,0:T(8,128)(2,1)}), bf16[8,16,768]{2,1,0:T(8,128)(2,1)}, u32[]{:S(2)}, u32[]{:S(2)}) async-start(bf16[8,16,768]{2,1,0:T(8,128)(2,1)} %bitcast.44), calls=%async_computation.2 | async-start | bytes 393216 | tf_op jit(solution)/shard_map/all_to_all | solution.py:103
  44.8 3.3 slice.103
  48.7 3.0 copy.25
  51.8 2.0 fusion.93
  53.8 2.5 reshape.178
  56.3 2.7 reshape.179
  59.4 1.5 fusion.17
  61.0 49.2 %all-reduce.11.cloned.1.call-done = f32[128,768]{1,0:T(8,128)} async-done(((f32[128,768]{1,0:T(8,128)}), f32[128,768]{1,0:T(8,128)}) %all-reduce.11.cloned.1.call-update) | async-done | bytes 393232 | tf_op jit(solution)/shard_map/psum | solution.py:110
  110.1 2.9 fusion.39
  113.1 3.5 fusion.25
  116.6 2.6 reshape.187
  119.2 2.8 fusion.23
  122.0 1.5 reshape_reshape.7
  123.4 2.4 gather_fusion.7
  125.9 5.6 %fusion.97 = f32[16,768,128]{2,1,0:T(8,128)} fusion(bf16[16,128,768]{2,1,0:T(8,128)(2,1)} %gather_fusion.7, bf16[16,128,128]{2,1,0:T(8,128)(2,1)S(1)} %copy-done), kind=kOutput, calls=%fused_computation.146 | convolution fusion | flops 402653184 | bytes 9961472 | tf_op jit(solution)/shard_map/tji,tjf->tif/dot_general | solution.py:33
  131.5 6.9 %copy.33 = f32[16,768,128]{1,0,2:T(8,128)} copy(f32[16,768,128]{2,1,0:T(8,128)} %fusion.97) | data formatting | bytes 12582912 | tf_op jit(solution)/shard_map/tji,tjf->tif/dot_general | solution.py:33
  138.3 4.6 fusion
  142.9 1.6 copy-done.2
  145.8 1.5 fusion.50
  147.3 2.3 slice.167
  150.3 3.8 all-to-all-start.3
  154.1 1.4 slice-done
  155.5 1.5 copy.26
  156.9 60.9 %all-reduce.13.cloned.1.call-done = f32[128,768]{1,0:T(8,128)} async-done(((f32[128,768]{1,0:T(8,128)}), f32[128,768]{1,0:T(8,128)}) %all-reduce.13.cloned.1.call-update) | async-done | bytes 393232 | tf_op jit(solution)/shard_map/psum | solution.py:110
  217.8 2.9 fusion.37
  220.8 3.4 fusion.24
  224.2 2.6 reshape.188
  226.8 2.0 convolution_add_fusion.3
  229.5 1.9 multiply_convert_fusion
  234.1 1.1 convolution_bitcast_fusion.6
  235.2 1.5 reshape.180
  237.6 40.3 %all-reduce.18 = bf16[128,768]{1,0:T(8,128)(2,1)} all-reduce(f32[128,768]{1,0:T(8,128)S(1)} %convert_select_fusion.1), channel_id=1, replica_groups=mesh['dom'=8,'batch'=4] {'dom'}, use_global_device_ids=true, to_apply=%region_0.1 | all-reduce | flops 98304 | bytes 589824 | tf_op jit(solution)/shard_map/psum | solution.py:93
  279.5 3.4 all-to-all-start
  286.7 4.0 all-to-all-done
  291.7 2.4 gather_fusion.2
  294.1 5.6 %fusion.94 = f32[16,768,128]{2,1,0:T(8,128)} fusion(bf16[16,128,768]{2,1,0:T(8,128)(2,1)} %gather_fusion.2, bf16[16,128,128]{2,1,0:T(8,128)(2,1)S(1)} %copy-done), kind=kOutput, calls=%fused_computation.143 | convolution fusion | flops 402653184 | bytes 9961472 | tf_op jit(solution)/shard_map/tij,tjf->tif/dot_general | solution.py:19
  299.7 6.9 %copy.30 = f32[16,768,128]{1,0,2:T(8,128)} copy(f32[16,768,128]{2,1,0:T(8,128)} %fusion.94) | data formatting | bytes 12582912 | tf_op jit(solution)/shard_map/tij,tjf->tif/dot_general | solution.py:19
  306.6 5.6 %fusion.26 = bf16[4,128,768]{2,0,1:T(4,128)(2,1)S(1)} fusion(f32[16,768,128]{1,0,2:T(8,128)} %copy.30, f32[16]{0:T(128)S(1)} %convert_element_type.95, s32[16]{0:T(128)S(1)} %copy-done.29), kind=kOutput, calls=%fused_computation.50 | convolution fusion | flops 77463616 | bytes 7078016 | tf_op jit(solution)/shard_map/rt,tif->rif/dot_general | solution.py:24
  312.3 1.5 gather_fusion.4
  315.1 1.2 convert_select_fusion
  317.1 3.4 all-to-all-start.1
  320.5 42.5 %all-reduce.19 = bf16[128,768]{1,0:T(8,128)(2,1)} all-reduce(f32[128,768]{1,0:T(8,128)S(1)} %convert_select_fusion), channel_id=1, replica_groups=mesh['dom'=8,'batch'=4] {'dom'}, use_global_device_ids=true, to_apply=%region_1.2 | all-reduce | flops 98304 | bytes 589824 | tf_op jit(solution)/shard_map/psum | solution.py:93
  365.1 2.4 gather_fusion.5
  367.6 5.6 %fusion.95 = f32[16,768,128]{2,1,0:T(8,128)} fusion(bf16[16,128,768]{2,1,0:T(8,128)(2,1)} %gather_fusion.5, bf16[16,128,128]{2,1,0:T(8,128)(2,1)S(1)} %copy-done), kind=kOutput, calls=%fused_computation.144 | convolution fusion | flops 402653184 | bytes 9961472 | tf_op jit(solution)/shard_map/tij,tjf->tif/dot_general | solution.py:19
  373.2 6.9 %copy.31 = f32[16,768,128]{1,0,2:T(8,128)} copy(f32[16,768,128]{2,1,0:T(8,128)} %fusion.95) | data formatting | bytes 12582912 | tf_op jit(solution)/shard_map/tij,tjf->tif/dot_general | solution.py:19
  380.1 5.6 %fusion.29 = bf16[4,128,768]{2,0,1:T(4,128)(2,1)S(1)} fusion(f32[16,768,128]{1,0,2:T(8,128)} %copy.31, f32[16]{0:T(128)S(1)} %convert_element_type.95, s32[16]{0:T(128)S(1)} %copy-done.29), kind=kOutput, calls=%fused_computation.51 | convolution fusion | flops 77463616 | bytes 7078016 | tf_op jit(solution)/shard_map/rt,tif->rif/dot_general | solution.py:24
  388.7 1.6 fusion.55
  390.3 42.5 %all-reduce.17.cloned.1.call-done = (f32[2,2,256,256]{2,3,1,0:T(8,128)}, f32[3,256,256]{2,1,0:T(8,128)}) async-done(((f32[2,2,256,256]{2,3,1,0:T(8,128)}, f32[3,256,256]{2,1,0:T(8,128)}), (f32[2,2,256,256]{2,3,1,0:T(8,128)}, f32[3,256,256]{2,1,0:T(8,128)})) %all-reduce.17.cloned.1.call-update) | async-done | bytes 1835024 | tf_op jit(solution)/shard_map/psum | solution.py:11
  432.8 3.2 convolution_add_fusion.1
  436.0 3.6 reshape.189
  440.8 1.6 fusion.16
  442.4 3.8 reshape.190
  446.1 3.5 fusion.32
  453.0 79.4 %all-reduce.15.cloned.1.call-done = (f32[2,2,256,256]{2,3,1,0:T(8,128)}, f32[3,256,256]{2,1,0:T(8,128)}) async-done(((f32[2,2,256,256]{2,3,1,0:T(8,128)}, f32[3,256,256]{2,1,0:T(8,128)}), (f32[2,2,256,256]{2,3,1,0:T(8,128)}, f32[3,256,256]{2,1,0:T(8,128)})) %all-reduce.15.cloned.1.call-update) | async-done | bytes 1835024 | tf_op jit(solution)/shard_map/psum | solution.py:12
  532.3 1.3 broadcast_multiply_fusion
  533.6 1.3 copy.29
  (130 shorter events, 29.6 us)
Async XLA Ops:
  7.2 6.8 %copy-start = (bf16[16,128,128]{2,1,0:T(8,128)(2,1)S(1)}, bf16[16,128,128]{2,1,0:T(8,128)(2,1)}, u32[]{:S(2)}) copy-start(bf16[16,128,128]{2,1,0:T(8,128)(2,1)} %param.18) | copy-start | bytes 1572868
  7.2 103.0 %all-reduce.11.cloned.1.call-start = ((), (), s32[]{:S(2)}) async-start(), calls=%async_computation.4 | async-start | bytes 786432 | tf_op jit(solution)/shard_map/psum | solution.py:110
  9.8 1.7 copy-start.29
  19.6 6.9 %copy-start.30 = (s32[16]{0:T(128)S(1)}, s32[16]{0:T(128)}, u32[]{:S(2)}) copy-start(s32[16]{0:T(128)} %param.21) | copy-start | bytes 196
  19.6 6.9 %copy-start.28 = (s32[16]{0:T(128)S(1)}, s32[16]{0:T(128)}, u32[]{:S(2)}) copy-start(s32[16]{0:T(128)} %param.20) | copy-start | bytes 196
  31.1 1.6 copy-start.1
  36.9 76.1 %all-to-all-start.2 = ((bf16[8,16,768]{2,1,0:T(8,128)(2,1)}), bf16[8,16,768]{2,1,0:T(8,128)(2,1)}, u32[]{:S(2)}, u32[]{:S(2)}) async-start(bf16[8,16,768]{2,1,0:T(8,128)(2,1)} %bitcast.44), calls=%async_computation.2 | async-start | bytes 393216 | tf_op jit(solution)/shard_map/all_to_all | solution.py:103
  44.3 173.6 %all-reduce.13.cloned.1.call-start = ((), (), s32[]{:S(2)}) async-start(), calls=%async_computation.5 | async-start | bytes 786432 | tf_op jit(solution)/shard_map/psum | solution.py:110
  44.8 3.4 copy-start.26
  44.8 3.5 copy-start.27
  44.8 3.7 copy-start.25
  44.8 3.7 copy-start.31
  48.7 3.1 copy-start.7
  53.8 5.2 copy-start.16
  56.3 3.1 copy-start.4
  142.9 1.6 copy-start.2
  150.3 70.5 %all-to-all-start.3 = ((bf16[8,16,768]{2,1,0:T(8,128)(2,1)}), bf16[8,16,768]{2,1,0:T(8,128)(2,1)S(1)}, u32[]{:S(2)}, u32[]{:S(2)}) async-start(bf16[8,16,768]{2,1,0:T(8,128)(2,1)} %bitcast.46), calls=%async_computation.3 | async-start | bytes 393216 | tf_op jit(solution)/shard_map/all_to_all | solution.py:103
  154.1 1.4 slice-start
  226.8 2.0 copy-start.5
  226.8 2.2 copy-start.18
  226.8 2.7 copy-start.20
  231.4 1.5 copy-start.12
  231.4 2.6 copy-start.8
  237.6 45.3 %copy-start.24 = (f32[1,256,256]{1,2,0:T(8,128)S(1)}, f32[1,256,256]{1,2,0:T(8,128)}, u32[]{:S(2)}) copy-start(f32[1,256,256]{1,2,0:T(8,128)} %convolution_bitcast_fusion.4) | copy-start | bytes 786436
  279.5 11.1 %all-to-all-start = ((bf16[8,16,768]{2,1,0:T(8,128)(2,1)}), bf16[8,16,768]{2,1,0:T(8,128)(2,1)S(1)}, u32[]{:S(2)}, u32[]{:S(2)}) async-start(bf16[8,16,768]{2,1,0:T(8,128)(2,1)} %broadcast_multiply_fusion.3), calls=%async_computation | async-start | bytes 393216 | tf_op jit(solution)/shard_map/all_to_all | solution.py:89
  284.1 1.5 copy-start.10
  315.0 49.1 %copy-start.14 = (bf16[1536,256]{1,0:T(8,128)(2,1)}, bf16[1536,256]{1,0:T(8,128)(2,1)S(1)}, u32[]{:S(2)}) copy-start(bf16[1536,256]{1,0:T(8,128)(2,1)S(1)} %convert_element_type.97) | copy-start | bytes 2359300
  317.1 47.1 %all-to-all-start.1 = ((bf16[8,16,768]{2,1,0:T(8,128)(2,1)}), bf16[8,16,768]{2,1,0:T(8,128)(2,1)S(1)}, u32[]{:S(2)}, u32[]{:S(2)}) async-start(bf16[8,16,768]{2,1,0:T(8,128)(2,1)} %broadcast_multiply_fusion.2), calls=%async_computation.1 | async-start | bytes 393216 | tf_op jit(solution)/shard_map/all_to_all | solution.py:89
  320.5 112.3 %all-reduce.17.cloned.1.call-start = ((), (), s32[]{:S(2)}) async-start(), calls=%async_computation.7 | async-start | bytes 3670016 | tf_op jit(solution)/shard_map/psum | solution.py:11
  386.1 1.0 copy-start.22
  386.1 1.0 copy-start.23
  387.1 1.4 copy-start.9
  387.2 1.6 copy-start.17
  388.1 144.2 %all-reduce.15.cloned.1.call-start = ((), (), s32[]{:S(2)}) async-start(), calls=%async_computation.6 | async-start | bytes 3670016 | tf_op jit(solution)/shard_map/psum | solution.py:12
  439.6 1.1 copy-start.13
  442.4 3.8 copy-start.3
  446.1 3.6 copy-start.6
  446.1 3.6 copy-start.11
  446.1 3.6 copy-start.19
  449.7 1.1 copy-start.15
  533.6 1.3 copy-start.21
Sparse Core Ops, SparseCore 0:
  34.0 76.0 all-reduce.10
  145.9 71.8 all-reduce.12
  388.2 44.5 all-reduce.16
  436.3 95.9 all-reduce.14
